TPU v7x, 32 devices: a whole 2x2x4 slice. The times are simulated.
32 devices in a mesh: row: 4 (over z), col: 4 (over x, core), tm: 2 (over y).
Axes of the slice: x: 2, y: 2, z: 4, core: 2. Of those that a mesh axis runs over, the one named last changes fastest.
Arguments:
- samples: bfloat16 [1024, 4, 2, 16384], P('row', None, 'tm', 'col'), may hold values from -6 to 6
- whitening: bfloat16 [1024, 1024], replicated, may hold values from -0.1875 to 0.1875
- ridge: float32 [2048], P('col'), may hold values from 2 to 20
- slab_start: int32 [1], replicated, may hold values from 0 to 63
- panels: int32 [4], replicated, may hold values from 0 to 3, as said below
Outputs:
- trailing: float32 [131072, 2048], P(('row', 'tm'), 'col')
- factor: bfloat16 [2, 131072, 512], P(None, ('row', 'tm'))
Inputs may be any that keep to these rules, and one draw needn't show every extreme that they name: `panels`: each panel index once.
All inputs are finite; a program needn't handle non-finite values.
Results may differ from a plain program's by a relative error of at most 0.012.
The roundings to bfloat16 on the way count: a program that leaves them out, or rounds other values in their place, can miss the bound.
Values may be sent and summed in bfloat16 or wider, within the bound.
A program may use at most 256 MiB of HBM per device.

v0:
```python
import jax
import jax.numpy as jnp
from jax import lax
from jax.sharding import PartitionSpec as P

S = 1024
PANEL = 512
PANELS = 2


def broadcast(block, axis, holder):
    block = jnp.where(lax.axis_index(axis) == holder, block, jnp.zeros_like(block))
    return lax.psum(block, axis)


def on_device(samples, whitening, ridge, slab_start, panels):
    moved = lax.all_to_all(samples, "row", split_axis=1, concat_axis=0, tiled=True)
    local_width = moved.shape[3]
    series = moved.reshape(moved.shape[0], local_width)
    whitened = jnp.dot(whitening, series, preferred_element_type=jnp.float32).astype(jnp.bfloat16)
    col_count = lax.axis_size("col")
    tm_count = lax.axis_size("tm")
    rows_here = col_count * local_width
    slab_width = PANEL * col_count
    scale = S ** (-0.5)
    slab_first = slab_start[0] * slab_width
    owner_index = slab_first // rows_here
    slab_offset = slab_first % rows_here
    col_index = lax.axis_index("col")
    self_index = lax.axis_index("row") * tm_count + lax.axis_index("tm")
    row_series = lax.all_gather(whitened, "col", axis=1, tiled=True)
    piece = lax.dynamic_slice_in_dim(row_series, slab_offset + col_index * PANEL, PANEL, 1)
    slab_part = broadcast(piece, ("row", "tm"), owner_index)
    covariance = (
        lax.dot_general(
            row_series, slab_part, (((0,), (0,)), ((), ())), preferred_element_type=jnp.float32
        )
        * scale
    )
    owner_flag = (self_index == owner_index).astype(jnp.float32)
    ridge_rows = slab_offset + col_index * PANEL
    zero_index = jnp.zeros((), jnp.int32)
    diag_block = (
        lax.dynamic_slice(covariance, (ridge_rows, zero_index), (PANEL, PANEL))
        + jnp.diag(ridge) * owner_flag
    )
    covariance = lax.dynamic_update_slice(covariance, diag_block, (ridge_rows, zero_index))
    identity = jnp.eye(PANEL, dtype=jnp.float32)
    factors = []
    finished = col_index < 0
    for section in range(PANELS):
        panel_index = panels[section]
        finished = finished | (col_index == panel_index)
        pivot_local = lax.dynamic_slice_in_dim(
            covariance, slab_offset + panel_index * PANEL, PANEL, 0
        )
        pivot_rows = broadcast(pivot_local, ("row", "tm"), owner_index)
        pivot_safe = jnp.where(col_index == panel_index, pivot_rows, identity)
        lower_factor = jnp.linalg.cholesky(pivot_safe)
        panel_now = jax.scipy.linalg.solve_triangular(lower_factor, covariance.T, lower=True).T
        small_block = lower_factor
        panel_bf = broadcast(panel_now.astype(jnp.bfloat16), "col", panel_index)
        small_block = broadcast(small_block, "col", panel_index)
        coupling = jax.scipy.linalg.solve_triangular(small_block, pivot_rows, lower=True).T
        coupling_bf = coupling.astype(jnp.bfloat16)
        covariance = covariance - lax.dot_general(
            panel_bf, coupling_bf, (((1,), (1,)), ((), ())), preferred_element_type=jnp.float32
        )
        factors.append(panel_bf)
    trailing = jnp.where(finished, jnp.zeros_like(covariance), covariance)
    return (trailing, jnp.stack(factors))


def solution(mesh):
    in_specs = (P("row", None, "tm", "col"), P(), P("col"), P(), P())
    out_specs = (P(("row", "tm"), "col"), P(None, ("row", "tm"), None))
    return jax.shard_map(
        on_device, mesh=mesh, in_specs=in_specs, out_specs=out_specs, check_vma=False
    )
```

profile of v0, /device:TPU:0, one launch (start us, length us, event | category | flops | bytes accessed | tf_op | source)
XLA Modules:
  0.0 1940.5 jit_solution(8248852513893661534)
XLA Ops:
  18.7 189.4 %all_to_all.15 = bf16[256,4,1,4096]{3,0,2,1:T(8,128)(2,1)S(1)} all-to-all(bf16[256,4,1,4096]{3,0,2,1:T(8,128)(2,1)} %copy.58), channel_id=1, replica_groups=mesh['row'=4,'col'=4,'tm'=2] {'row'}, dimensions={1} | all-to-all | bytes 16777216 | tf_op jit(solution)/shard_map/all_to_all | solution.py:17
  219.7 200.6 %all-gather.2.cloned.1.call-done = bf16[1024,16384]{1,0:T(8,128)(2,1)} async-done(((bf16[1024,4096]{1,0:T(8,128)(2,1)}), bf16[1024,16384]{1,0:T(8,128)(2,1)}) %all-gather.2.cloned.1.call-update) | async-done | bytes 33554448 | tf_op jit(solution)/shard_map/all_gather | solution.py:31
  424.6 78.0 %all-reduce.9.cloned.1.call-done = bf16[1024,512]{1,0:T(8,128)(2,1)} async-done(((bf16[1024,512]{1,0:T(8,128)(2,1)}), bf16[1024,512]{1,0:T(8,128)(2,1)}) %all-reduce.9.cloned.1.call-update) | async-done | bytes 1048592 | tf_op jit(solution)/shard_map/psum | solution.py:13
  502.6 31.8 %convolution_multiply_fusion = f32[16384,512]{0,1:T(8,128)} fusion(bf16[1024,16384]{1,0:T(8,128)(2,1)} %all-gather.2.cloned.1.call-done, bf16[1024,512]{1,0:T(8,128)(2,1)} %all-reduce.9.cloned.1.call-done), kind=kOutput, calls=%fused_computation.12 | convolution fusion | flops 17188257792 | bytes 68157440 | tf_op jit(solution)/shard_map/dot_general | solution.py:35
  545.4 77.0 %all-reduce.11.cloned.1.call-done = f32[512,512]{0,1:T(8,128)} async-done(((f32[512,512]{0,1:T(8,128)}), f32[512,512]{0,1:T(8,128)}) %all-reduce.11.cloned.1.call-update) | async-done | bytes 1048592 | tf_op jit(solution)/shard_map/psum | solution.py:13
  623.1 11.7 cholesky.286
  645.6 11.7 cholesky.305
  668.8 11.7 cholesky.326
  691.3 11.9 cholesky.343
  717.8 39.3 %custom-call.34 = f32[4,128,128]{1,2,0:T(8,128)S(1)} custom-call(f32[4,128,128]{2,1,0:T(8,128)S(1)} %get-tuple-element.33), custom_call_target="InvertDiagBlocksLowerTriangular" | custom-call | tf_op jit(solution)/shard_map/jit(_solve_triangular)/triangular_solve | solution.py:60
  767.0 12.8 convolution_subtract_fusion.4
  789.3 16.7 convolution_subtract_fusion.3
  817.7 22.9 %fusion.15 = f32[128,16384]{1,0:T(8,128)} fusion(f32[128,16384]{1,0:T(8,128)} %fusion.96, f32[128,16384]{1,0:T(8,128)} %fusion.98, f32[128,16384]{1,0:T(8,128)} %copy-done.2, f32[512,16384]{1,0:T(8,128)} %bitcast.173, f32[512,512]{0,1:T(8,128)S(1)} %get-tuple-element.357), kind=kOutput, calls=%fused_computation.31 | convolution fusion | flops 9678356480 | bytes 42139648 | tf_op jit(solution)/shard_map/jit(_solve_triangular)/triangular_solve | solution.py:60
  851.8 17.2 fusion.21
  879.6 39.3 %custom-call.35 = f32[4,128,128]{1,2,0:T(8,128)S(1)} custom-call(f32[4,128,128]{2,1,0:T(8,128)S(1)} %get-tuple-element.34), custom_call_target="InvertDiagBlocksLowerTriangular" | custom-call | tf_op jit(solution)/shard_map/jit(_solve_triangular)/triangular_solve | solution.py:64
  923.8 234.4 %all-reduce.13.cloned.1.call-done = bf16[16384,512]{0,1:T(8,128)(2,1)} async-done(((bf16[16384,512]{0,1:T(8,128)(2,1)}), bf16[16384,512]{0,1:T(8,128)(2,1)}) %all-reduce.13.cloned.1.call-update) | async-done | bytes 16777232 | tf_op jit(solution)/shard_map/psum | solution.py:13
  1158.2 28.8 %convolution_subtract_fusion = f32[16384,512]{0,1:T(8,128)} fusion(f32[16384,512]{0,1:T(8,128)} %dynamic_update_slice.3, bf16[16384,512]{0,1:T(8,128)(2,1)} %all-reduce.13.cloned.1.call-done, bf16[128,512]{1,0:T(8,128)(2,1)S(1)} %fusion.91, f32[128,512]{1,0:T(8,128)S(1)} %fusion.92, f32[128,512]{1,0:T(8,128)S(1)} %fusion.94, f32[128,512]{1,0:T(8,128)S(1)} %fusion.60), kind=kOutput, calls=%fused_computation.25 | convolution fusion | flops 8600420352 | bytes 84803584 | tf_op jit(solution)/shard_map/dot_general | solution.py:66
  1190.5 77.5 %all-reduce.17.cloned.1.call-done = f32[512,512]{0,1:T(8,128)} async-done(((f32[512,512]{0,1:T(8,128)}), f32[512,512]{0,1:T(8,128)}) %all-reduce.17.cloned.1.call-update) | async-done | bytes 1048592 | tf_op jit(solution)/shard_map/psum | solution.py:13
  1268.7 11.7 cholesky.358
  1291.2 11.7 cholesky.377
  1336.9 11.8 cholesky.415
  1363.9 39.3 %custom-call.39 = f32[4,128,128]{1,2,0:T(8,128)S(1)} custom-call(f32[4,128,128]{2,1,0:T(8,128)S(1)} %get-tuple-element.35), custom_call_target="InvertDiagBlocksLowerTriangular" | custom-call | tf_op jit(solution)/shard_map/jit(_solve_triangular)/triangular_solve | solution.py:60
  1413.1 12.8 convolution_subtract_fusion.2
  1435.4 16.6 convolution_subtract_fusion.1
  1463.7 22.9 %fusion.12 = f32[128,16384]{1,0:T(8,128)} fusion(f32[128,16384]{1,0:T(8,128)} %fusion.86, f32[128,16384]{1,0:T(8,128)} %fusion.88, f32[128,16384]{1,0:T(8,128)} %copy-done.3, f32[512,16384]{1,0:T(8,128)} %bitcast.169, f32[512,512]{0,1:T(8,128)S(1)} %get-tuple-element.358), kind=kOutput, calls=%fused_computation.30 | convolution fusion | flops 9678356480 | bytes 42139648 | tf_op jit(solution)/shard_map/jit(_solve_triangular)/triangular_solve | solution.py:60
  1497.8 17.2 fusion.19
  1524.7 39.5 %custom-call.40 = f32[4,128,128]{1,2,0:T(8,128)S(1)} custom-call(f32[4,128,128]{2,1,0:T(8,128)S(1)} %get-tuple-element.36), custom_call_target="InvertDiagBlocksLowerTriangular" | custom-call | tf_op jit(solution)/shard_map/jit(_solve_triangular)/triangular_solve | solution.py:64
  1569.0 234.4 %all-reduce.19.cloned.1.call-done = bf16[16384,512]{0,1:T(8,128)(2,1)} async-done(((bf16[16384,512]{0,1:T(8,128)(2,1)}), bf16[16384,512]{0,1:T(8,128)(2,1)}) %all-reduce.19.cloned.1.call-update) | async-done | bytes 16777232 | tf_op jit(solution)/shard_map/psum | solution.py:13
  1803.4 29.5 %subtract_select_fusion = f32[16384,512]{0,1:T(8,128)} fusion(f32[16384,512]{0,1:T(8,128)} %convolution_subtract_fusion, bf16[16384,512]{0,1:T(8,128)(2,1)} %all-reduce.19.cloned.1.call-done, pred[]{:T(512)S(6)} %or.26, bf16[128,512]{1,0:T(8,128)(2,1)S(1)} %fusion.81, f32[128,512]{1,0:T(8,128)S(1)} %fusion.82, f32[128,512]{1,0:T(8,128)S(1)} %fusion.84, ...), kind=kOutput, calls=%fused_computation.11 | convolution fusion | flops 8608808960 | bytes 84803584 | tf_op jit(solution)/shard_map/dot_general | solution.py:66
  1832.9 33.4 %copy.88 = f32[16384,512]{1,0:T(8,128)} copy(f32[16384,512]{0,1:T(8,128)} %subtract_select_fusion) | data formatting | bytes 67108864
  1866.3 23.0 %pad_maximum_fusion = bf16[2,16384,512]{1,2,0:T(8,128)(2,1)} fusion(bf16[1,16384,512]{1,2,0:T(8,128)(2,1)} %bitcast.175, bf16[1,16384,512]{1,2,0:T(8,128)(2,1)} %bitcast.174), kind=kLoop, calls=%fused_computation.10 | loop fusion | flops 16777216 | bytes 67108864 | tf_op jit(solution)/shard_map/stack | solution.py:71
  1889.3 44.1 %copy.89 = bf16[2,16384,512]{2,1,0:T(8,128)(2,1)} copy(bf16[2,16384,512]{1,2,0:T(8,128)(2,1)} %pad_maximum_fusion) | data formatting | bytes 67108864
  (224 shorter events, 289.8 us)
Async XLA Ops:
  7.2 200.9 %copy-start = (bf16[1024,1024]{1,0:T(8,128)(2,1)S(1)}, bf16[1024,1024]{1,0:T(8,128)(2,1)}, u32[]{:S(2)}) copy-start(bf16[1024,1024]{1,0:T(8,128)(2,1)} %param.11) | copy-start | bytes 6291460
  7.2 413.1 %all-gather.2.cloned.1.call-start = ((), (), s32[]{:S(2)}) async-start(), calls=%async_computation.1 | async-start | bytes 41943040 | tf_op jit(solution)/shard_map/all_gather | solution.py:31
  218.9 204.5 %copy-start.7 = (s32[4]{0:T(128)S(1)}, s32[4]{0:T(128)}, u32[]{:S(2)}) copy-start(s32[4]{0:T(128)} %param.14) | copy-start | bytes 52
  218.9 283.7 %all-reduce.9.cloned.1.call-start = ((), (), s32[]{:S(2)}) async-start(), calls=%async_computation.2 | async-start | bytes 2097152 | tf_op jit(solution)/shard_map/psum | solution.py:13
  423.1 199.3 %all-reduce.11.cloned.1.call-start = ((), (), s32[]{:S(2)}) async-start(), calls=%async_computation.3 | async-start | bytes 2097152 | tf_op jit(solution)/shard_map/psum | solution.py:13
  424.6 109.7 %copy-start.6 = (f32[512]{0:T(512)S(1)}, f32[512]{0:T(512)}, u32[]{:S(2)}) copy-start(f32[512]{0:T(512)} %param.12) | copy-start | bytes 6148
  544.5 325.2 %all-reduce.15.cloned.1.call-start = ((), (), s32[]{:S(2)}) async-start(), calls=%async_computation.5 | async-start | bytes 2097152 | tf_op jit(solution)/shard_map/psum | solution.py:13
  757.2 401.0 %all-reduce.13.cloned.1.call-start = ((), (), s32[]{:S(2)}) async-start(), calls=%async_computation.4 | async-start | bytes 33554432 | tf_op jit(solution)/shard_map/psum | solution.py:13
  767.0 12.8 copy-start.2
  868.9 50.0 %copy-start.4 = (f32[512,512]{0,1:T(8,128)S(1)}, f32[512,512]{0,1:T(8,128)}, u32[]{:S(2)}) copy-start(f32[512,512]{0,1:T(8,128)} %all-reduce.11.cloned.1.call-done) | copy-start | bytes 3145732
  869.0 399.0 %all-reduce.17.cloned.1.call-start = ((), (), s32[]{:S(2)}) async-start(), calls=%async_computation.6 | async-start | bytes 2097152 | tf_op jit(solution)/shard_map/psum | solution.py:13
  1189.6 325.4 %all-reduce.21.cloned.1.call-start = ((), (), s32[]{:S(2)}) async-start(), calls=%async_computation.8 | async-start | bytes 2097152 | tf_op jit(solution)/shard_map/psum | solution.py:13
  1403.2 400.1 %all-reduce.19.cloned.1.call-start = ((), (), s32[]{:S(2)}) async-start(), calls=%async_computation.7 | async-start | bytes 33554432 | tf_op jit(solution)/shard_map/psum | solution.py:13
  1413.0 12.8 copy-start.3
  1515.0 49.2 %copy-start.5 = (f32[512,512]{0,1:T(8,128)S(1)}, f32[512,512]{0,1:T(8,128)}, u32[]{:S(2)}) copy-start(f32[512,512]{0,1:T(8,128)} %all-reduce.17.cloned.1.call-done) | copy-start | bytes 3145732
  1889.3 44.1 %copy-start.1 = (bf16[1024,1024]{1,0:T(8,128)(2,1)S(1)}, bf16[1024,1024]{1,0:T(8,128)(2,1)}, u32[]{:S(2)}) copy-start(bf16[1024,1024]{1,0:T(8,128)(2,1)} %param.11) | copy-start | bytes 6291460
Sparse Core Ops, SparseCore 0:
  219.0 201.1 all-gather.1
  424.3 78.2 all-reduce.8
  544.6 77.7 all-reduce.10
  757.3 37.1 all-reduce.14
  869.1 289.0 all-reduce.12
  1189.7 78.1 all-reduce.16
  1403.4 36.2 all-reduce.20
  1515.1 288.2 all-reduce.18
where the time goes:
time: 1950 us; the launch traced here: 1940 us
  waiting for transfers between devices  902 us (46%)
  other arithmetic  389 us (20%)
  matrix products  304 us (16%)
  blocking collectives  189 us (10%)
  local copies, waits for them, and re-layouts  131 us (7%)
  between operations  23.4 us (1%)
    psum x7, waiting for transfers between devices, broadcast(): return lax.psum(block, axis)  701 us
    all_gather x1, waiting for transfers between devices, on_device(): row_series = lax.all_gather(whitened, 'col', axis=1, tiled=True)  201 us
    all_to_all x1, blocking collectives, on_device(): lax.all_to_all(samples, 'row', split_axis=1, concat_axis=0, tiled=True)  189 us
    another operation x14, matrix products, on_device(): jax.scipy.linalg.solve_triangular(lower_factor, covariance.T, lower=True)  189 us
    another operation x29, other arithmetic, on_device(): lower_factor = jnp.linalg.cholesky(pivot_safe)  159 us
    unnamed x19, local copies, waits for them, and re-layouts  89.1 us
    another operation x4, other arithmetic, on_device(): jax.scipy.linalg.solve_triangular(small_block, pivot_rows, lower=True)  81.5 us
    another operation x3, other arithmetic, on_device(): jax.scipy.linalg.solve_triangular(lower_factor, covariance.T, lower=True)  78.6 us
  transfers between devices with their start and end apart: 8, of which 6 were waited for; matrix products, arithmetic and copies ran while one was open for 17% of the time, Pallas kernels for 0%

commit v1 on v0

--- a/solution.py
+++ b/solution.py
@@ -14,7 +14,10 @@
 
 
 def on_device(samples, whitening, ridge, slab_start, panels):
-    moved = lax.all_to_all(samples, "row", split_axis=1, concat_axis=0, tiled=True)
+    moved = jnp.concatenate(
+        lax.all_to_all(jnp.stack(jnp.split(samples, lax.axis_size("row"), axis=1)), "row", 0, 0),
+        axis=0,
+    )
     local_width = moved.shape[3]
     series = moved.reshape(moved.shape[0], local_width)
     whitened = jnp.dot(whitening, series, preferred_element_type=jnp.float32).astype(jnp.bfloat16)

time: 1950 us -> 1970 us (1.010)
  local copies, waits for them, and re-layouts: 131 us -> 156 us
    split x0 -> x1, local copies, waits for them, and re-layouts: none -> 26.7 us  [on_device(): jnp.split(samples, lax.axis_size('row'), axis=1)]
    unnamed x19 -> x18, local copies, waits for them, and re-layouts: 89.1 us -> 77.6 us
    another operation x29 -> x30, other arithmetic: 159 us -> 159 us  [on_device(): lower_factor = jnp.linalg.cholesky(pivot_safe)]
where the time goes in v1:
time: 1970 us
  waiting for transfers between devices  903 us (46%)
  other arithmetic  391 us (20%)
  matrix products  304 us (15%)
  blocking collectives  189 us (10%)
  local copies, waits for them, and re-layouts  156 us (8%)
  between operations  23.4 us (1%)
    psum x7, waiting for transfers between devices, broadcast(): return lax.psum(block, axis)  702 us
    all_gather x1, waiting for transfers between devices, on_device(): row_series = lax.all_gather(whitened, 'col', axis=1, tiled=True)  201 us
    all_to_all x1, blocking collectives, on_device(): lax.all_to_all(jnp.stack(jnp.split(samples, lax.axis_size('row'), axis=1)...  189 us
    another operation x14, matrix products, on_device(): jax.scipy.linalg.solve_triangular(lower_factor, covariance.T, lower=True)  189 us
    another operation x30, other arithmetic, on_device(): lower_factor = jnp.linalg.cholesky(pivot_safe)  159 us
    another operation x4, other arithmetic, on_device(): jax.scipy.linalg.solve_triangular(small_block, pivot_rows, lower=True)  81.5 us
    another operation x3, other arithmetic, on_device(): jax.scipy.linalg.solve_triangular(lower_factor, covariance.T, lower=True)  78.6 us
    unnamed x18, local copies, waits for them, and re-layouts  77.6 us
  transfers between devices with their start and end apart: 8, of which 6 were waited for; matrix products, arithmetic and copies ran while one was open for 17% of the time, Pallas kernels for 0%

profile of v1, /device:TPU:0, one launch (start us, length us, event | category | flops | bytes accessed | tf_op | source)
XLA Modules:
  0.0 1967.6 jit_solution(542598669186948439)
XLA Ops:
  7.2 26.7 %fusion.121 = (bf16[256,1,1,4096]{3,1,2,0:T(2,128)(2,1)S(1)}, bf16[256,1,1,4096]{3,1,2,0:T(2,128)(2,1)S(1)}, bf16[256,1,1,4096]{3,1,2,0:T(2,128)(2,1)S(1)}, bf16[256,1,1,4096]{3,1,2,0:T(2,128)(2,1)S(1)}) fusion(bf16[256,4,1,4096]{3,1,2,0:T(4,128)(2,1)} %param.10), kind=kLoop, calls=%fused_computation.219 | loop fusion | bytes 16777216 | tf_op jit(solution)/shard_map/split | solution.py:18
  44.6 189.3 %all_to_all.5 = bf16[4,256,1,1,4096]{4,1,3,2,0:T(8,128)(2,1)S(1)} all-to-all(bf16[4,256,1,1,4096]{4,1,3,2,0:T(8,128)(2,1)S(1)} %pad_maximum_fusion.1), channel_id=1, replica_groups=mesh['row'=4,'col'=4,'tm'=2] {'row'}, dimensions={0} | all-to-all | bytes 16777216 | tf_op jit(solution)/shard_map/all_to_all | solution.py:18
  245.9 200.6 %all-gather.2.cloned.1.call-done = bf16[1024,16384]{0,1:T(8,128)(2,1)} async-done(((bf16[1024,4096]{0,1:T(8,128)(2,1)}), bf16[1024,16384]{0,1:T(8,128)(2,1)}) %all-gather.2.cloned.1.call-update) | async-done | bytes 33554448 | tf_op jit(solution)/shard_map/all_gather | solution.py:34
  450.4 78.4 %all-reduce.9.cloned.1.call-done = bf16[1024,512]{0,1:T(8,128)(2,1)} async-done(((bf16[1024,512]{0,1:T(8,128)(2,1)}), bf16[1024,512]{0,1:T(8,128)(2,1)}) %all-reduce.9.cloned.1.call-update) | async-done | bytes 1048592 | tf_op jit(solution)/shard_map/psum | solution.py:13
  528.8 31.8 %convolution_multiply_fusion = f32[16384,512]{0,1:T(8,128)} fusion(bf16[1024,16384]{0,1:T(8,128)(2,1)} %all-gather.2.cloned.1.call-done, bf16[1024,512]{0,1:T(8,128)(2,1)} %all-reduce.9.cloned.1.call-done), kind=kOutput, calls=%fused_computation.12 | convolution fusion | flops 17188257792 | bytes 68157440 | tf_op jit(solution)/shard_map/dot_general | solution.py:38
  571.7 77.1 %all-reduce.11.cloned.1.call-done = f32[512,512]{0,1:T(8,128)} async-done(((f32[512,512]{0,1:T(8,128)}), f32[512,512]{0,1:T(8,128)}) %all-reduce.11.cloned.1.call-update) | async-done | bytes 1048592 | tf_op jit(solution)/shard_map/psum | solution.py:13
  649.5 11.7 cholesky.286
  672.0 11.7 cholesky.305
  695.2 11.7 cholesky.326
  717.6 11.9 cholesky.343
  744.8 39.3 %custom-call.34 = f32[4,128,128]{1,2,0:T(8,128)S(1)} custom-call(f32[4,128,128]{2,1,0:T(8,128)S(1)} %get-tuple-element.33), custom_call_target="InvertDiagBlocksLowerTriangular" | custom-call | tf_op jit(solution)/shard_map/jit(_solve_triangular)/triangular_solve | solution.py:63
  794.0 12.8 convolution_subtract_fusion.4
  816.3 16.7 convolution_subtract_fusion.3
  844.7 22.9 %fusion.15 = f32[128,16384]{1,0:T(8,128)} fusion(f32[128,16384]{1,0:T(8,128)} %fusion.96, f32[128,16384]{1,0:T(8,128)} %fusion.98, f32[128,16384]{1,0:T(8,128)} %copy-done.2, f32[512,16384]{1,0:T(8,128)} %bitcast.179, f32[512,512]{0,1:T(8,128)S(1)} %get-tuple-element.345), kind=kOutput, calls=%fused_computation.31 | convolution fusion | flops 9678356480 | bytes 42139648 | tf_op jit(solution)/shard_map/jit(_solve_triangular)/triangular_solve | solution.py:63
  878.8 17.2 fusion.21
  906.7 39.3 %custom-call.35 = f32[4,128,128]{1,2,0:T(8,128)S(1)} custom-call(f32[4,128,128]{2,1,0:T(8,128)S(1)} %get-tuple-element.34), custom_call_target="InvertDiagBlocksLowerTriangular" | custom-call | tf_op jit(solution)/shard_map/jit(_solve_triangular)/triangular_solve | solution.py:67
  950.8 234.4 %all-reduce.13.cloned.1.call-done = bf16[16384,512]{0,1:T(8,128)(2,1)} async-done(((bf16[16384,512]{0,1:T(8,128)(2,1)}), bf16[16384,512]{0,1:T(8,128)(2,1)}) %all-reduce.13.cloned.1.call-update) | async-done | bytes 16777232 | tf_op jit(solution)/shard_map/psum | solution.py:13
  1185.2 28.8 %convolution_subtract_fusion = f32[16384,512]{0,1:T(8,128)} fusion(f32[16384,512]{0,1:T(8,128)} %dynamic_update_slice.3, bf16[16384,512]{0,1:T(8,128)(2,1)} %all-reduce.13.cloned.1.call-done, bf16[128,512]{1,0:T(8,128)(2,1)S(1)} %fusion.91, f32[128,512]{1,0:T(8,128)S(1)} %fusion.92, f32[128,512]{1,0:T(8,128)S(1)} %fusion.94, f32[128,512]{1,0:T(8,128)S(1)} %fusion.60), kind=kOutput, calls=%fused_computation.25 | convolution fusion | flops 8600420352 | bytes 84803584 | tf_op jit(solution)/shard_map/dot_general | solution.py:69
  1217.5 77.6 %all-reduce.17.cloned.1.call-done = f32[512,512]{0,1:T(8,128)} async-done(((f32[512,512]{0,1:T(8,128)}), f32[512,512]{0,1:T(8,128)}) %all-reduce.17.cloned.1.call-update) | async-done | bytes 1048592 | tf_op jit(solution)/shard_map/psum | solution.py:13
  1295.8 11.7 cholesky.358
  1364.0 11.8 cholesky.415
  1391.0 39.3 %custom-call.39 = f32[4,128,128]{1,2,0:T(8,128)S(1)} custom-call(f32[4,128,128]{2,1,0:T(8,128)S(1)} %get-tuple-element.35), custom_call_target="InvertDiagBlocksLowerTriangular" | custom-call | tf_op jit(solution)/shard_map/jit(_solve_triangular)/triangular_solve | solution.py:63
  1440.2 12.8 convolution_subtract_fusion.2
  1462.5 16.6 convolution_subtract_fusion.1
  1490.8 22.9 %fusion.12 = f32[128,16384]{1,0:T(8,128)} fusion(f32[128,16384]{1,0:T(8,128)} %fusion.86, f32[128,16384]{1,0:T(8,128)} %fusion.88, f32[128,16384]{1,0:T(8,128)} %copy-done.3, f32[512,16384]{1,0:T(8,128)} %bitcast.175, f32[512,512]{0,1:T(8,128)S(1)} %get-tuple-element.346), kind=kOutput, calls=%fused_computation.30 | convolution fusion | flops 9678356480 | bytes 42139648 | tf_op jit(solution)/shard_map/jit(_solve_triangular)/triangular_solve | solution.py:63
  1524.9 17.2 fusion.19
  1551.8 39.5 %custom-call.40 = f32[4,128,128]{1,2,0:T(8,128)S(1)} custom-call(f32[4,128,128]{2,1,0:T(8,128)S(1)} %get-tuple-element.36), custom_call_target="InvertDiagBlocksLowerTriangular" | custom-call | tf_op jit(solution)/shard_map/jit(_solve_triangular)/triangular_solve | solution.py:67
  1596.1 234.4 %all-reduce.19.cloned.1.call-done = bf16[16384,512]{0,1:T(8,128)(2,1)} async-done(((bf16[16384,512]{0,1:T(8,128)(2,1)}), bf16[16384,512]{0,1:T(8,128)(2,1)}) %all-reduce.19.cloned.1.call-update) | async-done | bytes 16777232 | tf_op jit(solution)/shard_map/psum | solution.py:13
  1830.5 29.5 %subtract_select_fusion = f32[16384,512]{0,1:T(8,128)} fusion(f32[16384,512]{0,1:T(8,128)} %convolution_subtract_fusion, bf16[16384,512]{0,1:T(8,128)(2,1)} %all-reduce.19.cloned.1.call-done, pred[]{:T(512)S(6)} %or.26, bf16[128,512]{1,0:T(8,128)(2,1)S(1)} %fusion.81, f32[128,512]{1,0:T(8,128)S(1)} %fusion.82, f32[128,512]{1,0:T(8,128)S(1)} %fusion.84, ...), kind=kOutput, calls=%fused_computation.11 | convolution fusion | flops 8608808960 | bytes 84803584 | tf_op jit(solution)/shard_map/dot_general | solution.py:69
  1860.0 33.4 %copy.62 = f32[16384,512]{1,0:T(8,128)} copy(f32[16384,512]{0,1:T(8,128)} %subtract_select_fusion) | data formatting | bytes 67108864
  1893.4 23.0 %pad_maximum_fusion = bf16[2,16384,512]{1,2,0:T(8,128)(2,1)} fusion(bf16[1,16384,512]{1,2,0:T(8,128)(2,1)} %bitcast.181, bf16[1,16384,512]{1,2,0:T(8,128)(2,1)} %bitcast.180), kind=kLoop, calls=%fused_computation.10 | loop fusion | flops 16777216 | bytes 67108864 | tf_op jit(solution)/shard_map/stack | solution.py:74
  1916.4 44.1 %copy.63 = bf16[2,16384,512]{2,1,0:T(8,128)(2,1)} copy(bf16[2,16384,512]{1,2,0:T(8,128)(2,1)} %pad_maximum_fusion) | data formatting | bytes 67108864
  (228 shorter events, 301.2 us)
Async XLA Ops:
  7.2 226.8 %copy-start = (bf16[1024,1024]{1,0:T(8,128)(2,1)S(1)}, bf16[1024,1024]{1,0:T(8,128)(2,1)}, u32[]{:S(2)}) copy-start(bf16[1024,1024]{1,0:T(8,128)(2,1)} %param.11) | copy-start | bytes 6291460
  7.2 439.3 %all-gather.2.cloned.1.call-start = ((), (), s32[]{:S(2)}) async-start(), calls=%async_computation.1 | async-start | bytes 41943040 | tf_op jit(solution)/shard_map/all_gather | solution.py:34
  245.2 204.0 %copy-start.7 = (s32[4]{0:T(128)S(1)}, s32[4]{0:T(128)}, u32[]{:S(2)}) copy-start(s32[4]{0:T(128)} %param.14) | copy-start | bytes 52
  245.2 283.6 %all-reduce.9.cloned.1.call-start = ((), (), s32[]{:S(2)}) async-start(), calls=%async_computation.2 | async-start | bytes 2097152 | tf_op jit(solution)/shard_map/psum | solution.py:13
  449.1 199.7 %all-reduce.11.cloned.1.call-start = ((), (), s32[]{:S(2)}) async-start(), calls=%async_computation.3 | async-start | bytes 2097152 | tf_op jit(solution)/shard_map/psum | solution.py:13
  450.4 110.2 %copy-start.6 = (f32[512]{0:T(512)S(1)}, f32[512]{0:T(512)}, u32[]{:S(2)}) copy-start(f32[512]{0:T(512)} %param.12) | copy-start | bytes 6148
  570.7 326.0 %all-reduce.15.cloned.1.call-start = ((), (), s32[]{:S(2)}) async-start(), calls=%async_computation.5 | async-start | bytes 2097152 | tf_op jit(solution)/shard_map/psum | solution.py:13
  784.2 401.0 %all-reduce.13.cloned.1.call-start = ((), (), s32[]{:S(2)}) async-start(), calls=%async_computation.4 | async-start | bytes 33554432 | tf_op jit(solution)/shard_map/psum | solution.py:13
  794.0 12.8 copy-start.2
  895.9 50.0 %copy-start.4 = (f32[512,512]{0,1:T(8,128)S(1)}, f32[512,512]{0,1:T(8,128)}, u32[]{:S(2)}) copy-start(f32[512,512]{0,1:T(8,128)} %all-reduce.11.cloned.1.call-done) | copy-start | bytes 3145732
  896.0 399.1 %all-reduce.17.cloned.1.call-start = ((), (), s32[]{:S(2)}) async-start(), calls=%async_computation.6 | async-start | bytes 2097152 | tf_op jit(solution)/shard_map/psum | solution.py:13
  1216.6 325.5 %all-reduce.21.cloned.1.call-start = ((), (), s32[]{:S(2)}) async-start(), calls=%async_computation.8 | async-start | bytes 2097152 | tf_op jit(solution)/shard_map/psum | solution.py:13
  1430.3 400.1 %all-reduce.19.cloned.1.call-start = ((), (), s32[]{:S(2)}) async-start(), calls=%async_computation.7 | async-start | bytes 33554432 | tf_op jit(solution)/shard_map/psum | solution.py:13
  1440.1 12.8 copy-start.3
  1542.1 49.2 %copy-start.5 = (f32[512,512]{0,1:T(8,128)S(1)}, f32[512,512]{0,1:T(8,128)}, u32[]{:S(2)}) copy-start(f32[512,512]{0,1:T(8,128)} %all-reduce.17.cloned.1.call-done) | copy-start | bytes 3145732
  1916.4 44.1 %copy-start.1 = (bf16[1024,1024]{1,0:T(8,128)(2,1)S(1)}, bf16[1024,1024]{1,0:T(8,128)(2,1)}, u32[]{:S(2)}) copy-start(bf16[1024,1024]{1,0:T(8,128)(2,1)} %param.11) | copy-start | bytes 6291460
Sparse Core Ops, SparseCore 0:
  245.3 201.1 all-gather.1
  450.6 78.2 all-reduce.8
  570.9 77.8 all-reduce.10
  784.3 37.1 all-reduce.14
  896.1 289.0 all-reduce.12
  1216.8 78.2 all-reduce.16
  1430.5 36.2 all-reduce.20
  1542.2 288.2 all-reduce.18
